TPU v7x, 128 devices: a whole 4x4x4 slice. The times are simulated.
128 devices in a mesh: seq: 64 (over y, z, x), ch: 2 (over core).
Axes of the slice: x: 4, y: 4, z: 4, core: 2. Of those that a mesh axis runs over, the one named last changes fastest.
Arguments:
- cotangent: bfloat16 [16384, 2, 2048], P('seq', None, 'ch'), may hold values from -6 to 6
- conv_input: bfloat16 [16384, 2, 2048], P('seq', None, 'ch'), may hold values from -6 to 6
- decay_rate: bfloat16 [16384, 2048], P('seq', 'ch'), may hold values from 2.4414063e-06 to 0.7
- angle: float32 [2048], P('ch'), may hold values from -3.140625 to 3.140625
- conv_weight: float32 [4, 2, 2048], P(None, None, 'ch'), may hold values from -3 to 3
- in_weight: bfloat16 [4096, 2, 2048], P(None, None, 'ch'), may hold values from -0.09375 to 0.09375
Outputs:
- input_grad: bfloat16 [16384, 4096], P(('seq', 'ch'))
- channel_major: bfloat16 [2, 2048, 16384], P(None, ('ch', 'seq'))
- tap_grad: float32 [4, 2, 2048], P(None, None, 'ch')
All inputs are finite; a program needn't handle non-finite values.
Results may differ from a plain program's by a relative error of at most 0.0085.
Values may be sent and summed in bfloat16 or wider, within the bound.
A program may use at most 128 MiB of HBM per device.

v0:
```python
import jax
import jax.numpy as jnp
from jax import lax
from jax.sharding import PartitionSpec as P


def prefix(value, axis, join, neutral):
    count, mine = (lax.axis_size(axis), lax.axis_index(axis))
    pieces = jax.tree.map(lambda part: lax.all_gather(part, axis), value)
    pieces = jax.tree.map(lambda part: part[::-1], pieces)
    mine = count - 1 - mine
    total = jax.tree.map(
        lambda part, zero: jnp.full_like(part, 0) + jnp.asarray(zero, part.dtype), value, neutral
    )

    def hop(position, total):
        longer = join(total, jax.tree.map(lambda part: part[position], pieces))
        return jax.tree.map(lambda new, old: jnp.where(position < mine, new, old), longer, total)

    return lax.fori_loop(0, count - 1, hop, total)


def passed_along(array, axis, by):
    count = lax.axis_size(axis)
    pairs = [(i, i + by) for i in range(count) if 0 <= i + by < count]
    return lax.ppermute(array, axis, pairs)


def compose(earlier, later):
    outer_real, outer_imag, outer_shift_real, outer_shift_imag = earlier
    inner_real, inner_imag, inner_shift_real, inner_shift_imag = later
    return (
        inner_real * outer_real - inner_imag * outer_imag,
        inner_real * outer_imag + inner_imag * outer_real,
        inner_real * outer_shift_real - inner_imag * outer_shift_imag + inner_shift_real,
        inner_real * outer_shift_imag + inner_imag * outer_shift_real + inner_shift_imag,
    )


def local_block(cotangent, decay_rate, angle):
    rates = decay_rate.astype(jnp.float32)
    modulus = jnp.exp(-rates)
    mult_real = modulus * jnp.cos(angle)[None, :]
    mult_imag = -modulus * jnp.sin(angle)[None, :]
    step_real = jnp.concatenate([mult_real[1:], jnp.ones_like(mult_real[:1])], 0)
    step_imag = jnp.concatenate([mult_imag[1:], jnp.zeros_like(mult_imag[:1])], 0)
    upstream = cotangent.astype(jnp.float32)
    elements = (step_real[::-1], step_imag[::-1], upstream[::-1, 0], upstream[::-1, 1])
    scanned = lax.associative_scan(compose, elements, axis=0)
    prod_real, prod_imag, base_real, base_imag = [member[::-1] for member in scanned]
    return (rates, mult_real, mult_imag, prod_real, prod_imag, base_real, base_imag)


def on_device(cotangent, conv_input, decay_rate, angle, conv_weight, in_weight):
    rates, mult_real, mult_imag, prod_real, prod_imag, base_real, base_imag = local_block(
        cotangent, decay_rate, angle
    )
    length = cotangent.shape[0]
    width = cotangent.shape[2]
    map_real = mult_real[0] * prod_real[0] - mult_imag[0] * prod_imag[0]
    map_imag = mult_real[0] * prod_imag[0] + mult_imag[0] * prod_real[0]
    shift_real = mult_real[0] * base_real[0] - mult_imag[0] * base_imag[0]
    shift_imag = mult_real[0] * base_imag[0] + mult_imag[0] * base_real[0]
    ones_vec = jnp.ones((width,), jnp.float32)
    zero_vec = jnp.zeros((width,), jnp.float32)
    carried = prefix(
        (map_real, map_imag, shift_real, shift_imag),
        "seq",
        compose,
        (ones_vec, zero_vec, zero_vec, zero_vec),
    )
    carry_real = carried[2]
    carry_imag = carried[3]
    grad_real = base_real + prod_real * carry_real[None] - prod_imag * carry_imag[None]
    grad_imag = base_imag + prod_real * carry_imag[None] + prod_imag * carry_real[None]
    scaling = jnp.sqrt(-jnp.expm1(-2.0 * rates))
    conv_grad = jnp.stack([grad_real * scaling, grad_imag * scaling], 1)
    upper_rim = passed_along(conv_grad[:3], "seq", -1)
    extended = jnp.concatenate([conv_grad, upper_rim], 0)
    feature_sum = conv_weight[0][None] * extended[0:length]
    for tap_index in range(1, 4):
        feature_sum = (
            feature_sum + conv_weight[tap_index][None] * extended[tap_index : tap_index + length]
        )
    input_feat = feature_sum.astype(jnp.bfloat16)
    lower_rim = passed_along(conv_input[length - 3 :], "seq", 1)
    shifted_input = jnp.concatenate([lower_rim, conv_input], 0).astype(jnp.float32)
    taps = []
    for tap_index in range(4):
        taps.append(
            jnp.sum(conv_grad * shifted_input[3 - tap_index : 3 - tap_index + length], axis=0)
        )
    tap_grad = lax.psum(jnp.stack(taps, 0), "seq")
    layout = jnp.transpose(input_feat, (1, 2, 0))
    channel_major = lax.all_to_all(layout, "seq", split_axis=1, concat_axis=2, tiled=True)
    summed = lax.psum_scatter(
        lax.dot_general(
            input_feat, in_weight, (((1, 2), (1, 2)), ((), ())), preferred_element_type=jnp.float32
        ).astype(jnp.bfloat16),
        "ch",
        scatter_dimension=0,
        tiled=True,
    )
    return (summed, channel_major, tap_grad)


def solution(mesh):
    in_specs = (
        P("seq", None, "ch"),
        P("seq", None, "ch"),
        P("seq", "ch"),
        P("ch"),
        P(None, None, "ch"),
        P(None, None, "ch"),
    )
    out_specs = (P(("seq", "ch"), None), P(None, ("ch", "seq"), None), P(None, None, "ch"))
    return jax.shard_map(
        on_device, mesh=mesh, in_specs=in_specs, out_specs=out_specs, check_vma=False
    )
```

profile of v0, /device:TPU:0, one launch (start us, length us, event | category | flops | bytes accessed | tf_op | source)
XLA Modules:
  0.0 1332.5 jit_solution(1409491636093875351)
XLA Ops:
  8.5 4.1 collective-permute-start.1
  33.6 2.7 slice.587
  36.2 2.7 slice.576
  38.9 2.6 slice.581
  41.5 2.7 slice.589
  89.0 4.6 pad.263
  103.1 4.6 pad.260
  111.9 8.9 rev.34
  120.9 5.2 rev.41
  126.1 176.5 %all-gather.3 = f32[64,1,1024]{2,1,0:T(1,128)S(1)} all-gather(f32[1,1,1024]{2,1,0:T(1,128)S(1)} %get-tuple-element.198), channel_id=1, replica_groups=mesh['seq'=64,'ch'=2] {'seq'}, dimensions={0}, use_global_device_ids=true | all-gather | bytes 266240 | tf_op jit(solution)/shard_map/all_gather | solution.py:9
  302.7 2.6 rev.39
  305.3 170.6 %all-gather.2 = f32[64,1,1024]{2,1,0:T(1,128)S(1)} all-gather(f32[1,1,1024]{2,1,0:T(1,128)S(1)} %get-tuple-element.199), channel_id=1, replica_groups=mesh['seq'=64,'ch'=2] {'seq'}, dimensions={0}, use_global_device_ids=true | all-gather | bytes 266240 | tf_op jit(solution)/shard_map/all_gather | solution.py:9
  476.0 2.5 rev.38
  479.1 5.2 rev.40
  484.3 172.6 %all-gather.1 = f32[64,1,1024]{2,1,0:T(1,128)S(1)} all-gather(f32[1,1,1024]{2,1,0:T(1,128)S(1)} %get-tuple-element.200), channel_id=1, replica_groups=mesh['seq'=64,'ch'=2] {'seq'}, dimensions={0}, use_global_device_ids=true | all-gather | bytes 266240 | tf_op jit(solution)/shard_map/all_gather | solution.py:9
  656.9 2.5 rev.37
  659.5 170.6 %all-gather = f32[64,1,1024]{2,1,0:T(1,128)S(1)} all-gather(f32[1,1,1024]{2,1,0:T(1,128)S(1)} %get-tuple-element.201), channel_id=1, replica_groups=mesh['seq'=64,'ch'=2] {'seq'}, dimensions={0}, use_global_device_ids=true | all-gather | bytes 266240 | tf_op jit(solution)/shard_map/all_gather | solution.py:9
  832.7 102.7 %while.16 = (s32[]{:T(128)}, f32[1024]{0:T(1024)S(1)}, f32[1024]{0:T(1024)S(1)}, s32[]{:T(128)}, f32[64,1024]{1,0:T(8,128)}, /*index=5*/f32[64,1024]{1,0:T(8,128...) while((s32[]{:T(128)}, f32[1024]{0:T(1024)S(1)}, f32[1024]{0:T(1024)S(1)}, ...), condition=%wide.region_1.2_spmd.clone, body=%wide.region_0.1_spmd.clone.sunk | while | flops 12292 | bytes 65673 | solution.py:20
  942.8 2.6 collective-permute-done
  947.3 8.0 fusion.11
  955.2 12.7 fusion.5
  967.9 3.1 copy.31
  971.0 4.7 all-to-all-start
  975.7 348.7 %psum.7 = f32[4,2,1024]{2,1,0:T(2,128)} all-reduce(f32[4,2,1024]{2,1,0:T(2,128)S(1)} %pad_maximum_fusion.20), channel_id=1, replica_groups=mesh['seq'=64,'ch'=2] {'seq'}, use_global_device_ids=true, to_apply=%region_7.8 | all-reduce | flops 8192 | bytes 65536 | tf_op jit(solution)/shard_map/psum | solution.py:93
  (550 shorter events, 193.6 us)
Async XLA Ops:
  7.2 1318.5 %reduce-scatter.2.cloned.1.call-start = ((), (), s32[]{:S(2)}) async-start(), calls=%async_computation.2 | async-start | bytes 3145728 | tf_op jit(solution)/shard_map/reduce_scatter | solution.py:96
  8.5 932.4 %collective-permute-start.1 = (bf16[3,2,1024]{2,1,0:T(2,128)(2,1)}, bf16[3,2,1024]{2,1,0:T(2,128)(2,1)}, u32[]{:S(2)}, u32[]{:S(2)}) collective-permute-start(bf16[3,2,1024]{2,1,0:T(2,128)(2,1)} %slice.741), channel_id=1, source_target_pairs={{0,2},{2,4},{4,6},{6,8},{8,10},{10,12},{12,14},{14,16},{16,18},{18... | collective-permute-start | bytes 36872 | tf_op jit(solution)/shard_map/ppermute | solution.py:26
  14.7 5.5 copy-start.5
  20.4 4.4 copy-start.24
  29.1 4.4 copy-start.19
  29.1 7.1 copy-start.18
  33.5 5.3 copy-start.21
  33.6 8.0 copy-start.20
  61.9 4.8 copy-start.33
  62.7 4.0 copy-start.35
  62.7 4.0 copy-start.39
  67.6 4.0 copy-start.25
  67.6 4.0 copy-start.26
  71.8 4.2 copy-start.30
  71.9 5.8 copy-start.29
  74.2 5.2 copy-start.28
  74.3 5.2 copy-start.27
  110.8 10.1 copy-start.6
  120.9 357.6 %copy-start.8 = (f32[256,1024]{1,0:T(8,128)S(1)}, f32[256,1024]{1,0:T(8,128)}, u32[]{:S(2)}) copy-start(f32[256,1024]{1,0:T(8,128)} %add.573) | copy-start | bytes 3145732
  302.7 176.3 %copy-start.7 = (f32[256,1024]{1,0:T(8,128)S(1)}, f32[256,1024]{1,0:T(8,128)}, u32[]{:S(2)}) copy-start(f32[256,1024]{1,0:T(8,128)} %add.575) | copy-start | bytes 3145732
  484.2 451.1 %copy-start.9 = (f32[256,1024]{1,0:T(8,128)S(1)}, f32[256,1024]{1,0:T(8,128)}, u32[]{:S(2)}) copy-start(f32[256,1024]{1,0:T(8,128)} %rev.34) | copy-start | bytes 3145732
  484.3 451.1 %copy-start.10 = (f32[256,1024]{1,0:T(8,128)S(1)}, f32[256,1024]{1,0:T(8,128)}, u32[]{:S(2)}) copy-start(f32[256,1024]{1,0:T(8,128)} %rev.41) | copy-start | bytes 3145732
  939.6 5.7 collective-permute-start
  971.0 353.4 %all-to-all-start = ((bf16[2,1024,256]{2,0,1:T(2,128)(2,1)}), bf16[2,1024,256]{2,0,1:T(2,128)(2,1)S(1)}, u32[]{:S(2)}, u32[]{:S(2)}) async-start(bf16[2,1024,256]{2,0,1:T(2,128)(2,1)} %copy.31), calls=%async_computation.1 | async-start | bytes 2097152 | tf_op jit(solution)/shard_map/all_to_all | solution.py:95
  (23 other events, 42.4 us)
Sparse Core Ops, SparseCore 0:
  968.0 7.8 reduce-scatter.1
where the time goes:
time: 1340 us; the launch traced here: 1330 us
  blocking collectives  1040 us (78%)
  local copies, waits for them, and re-layouts  205 us (15%)
  other arithmetic  44.8 us (3%)
  between operations  15.7 us (1%)
    all_gather x4, blocking collectives, prefix(): pieces = jax.tree.map(lambda part: lax.all_gather(part, axis), value)  690 us
    psum x1, blocking collectives, on_device(): tap_grad = lax.psum(jnp.stack(taps, 0), 'seq')  349 us
    dynamic_slice x126, local copies, waits for them, and re-layouts, hop(): longer = join(total, jax.tree.map(lambda part: part[position], pieces))  99.6 us
    slice x110, local copies, waits for them, and re-layouts, local_block(): scanned = lax.associative_scan(compose, elements, axis=0)  36.3 us
  transfers between devices with their start and end apart: 4, of which 1 were waited for; matrix products, arithmetic and copies ran while one was open for 18% of the time, Pallas kernels for 0%

commit v1 on v0

--- a/solution.py
+++ b/solution.py
@@ -90,7 +90,7 @@
         taps.append(
             jnp.sum(conv_grad * shifted_input[3 - tap_index : 3 - tap_index + length], axis=0)
         )
-    tap_grad = lax.psum(jnp.stack(taps, 0), "seq")
+    tap_grad = jnp.sum(lax.all_gather(jnp.stack(taps, 0), "seq"), axis=0)
     layout = jnp.transpose(input_feat, (1, 2, 0))
     channel_major = lax.all_to_all(layout, "seq", split_axis=1, concat_axis=2, tiled=True)
     summed = lax.psum_scatter(

time: 1340 us -> 1040 us (0.78)
  blocking collectives: 1040 us -> 710 us
  waiting for transfers between devices: 2.59 us -> 28.1 us
    psum x1 -> x0, blocking collectives: 349 us -> none  [on_device(): tap_grad = lax.psum(jnp.stack(taps, 0), 'seq')]
    all_gather x0 -> x1, waiting for transfers between devices: none -> 25.5 us  [on_device(): tap_grad = jnp.sum(lax.all_gather(jnp.stack(taps, 0), 'seq'), axis=0)]
    all_to_all x0 -> x1, blocking collectives: none -> 19.3 us  [on_device(): lax.all_to_all(layout, 'seq', split_axis=1, concat_axis=2, tiled=True)]
  transfers between devices with their start and end apart: 4 -> 4, of which waited for: 1 -> 2; matrix products, arithmetic and copies ran while one was open for 18% -> 24% of each run, Pallas kernels for 0% -> 0%
where the time goes in v1:
time: 1040 us; the launch traced here: 1030 us
  blocking collectives  710 us (68%)
  local copies, waits for them, and re-layouts  205 us (20%)
  other arithmetic  48.4 us (5%)
  waiting for transfers between devices  28.1 us (3%)
  between operations  17.1 us (2%)
  matrix products  12.7 us (1%)
    all_gather x4, blocking collectives, prefix(): pieces = jax.tree.map(lambda part: lax.all_gather(part, axis), value)  690 us
    dynamic_slice x126, local copies, waits for them, and re-layouts, hop(): longer = join(total, jax.tree.map(lambda part: part[position], pieces))  99.6 us
    slice x110, local copies, waits for them, and re-layouts, local_block(): scanned = lax.associative_scan(compose, elements, axis=0)  36.4 us
    all_gather x1, waiting for transfers between devices, on_device(): tap_grad = jnp.sum(lax.all_gather(jnp.stack(taps, 0), 'seq'), axis=0)  25.5 us
    pad x56, local copies, waits for them, and re-layouts, local_block(): scanned = lax.associative_scan(compose, elements, axis=0)  24.1 us
  transfers between devices with their start and end apart: 4, of which 2 were waited for; matrix products, arithmetic and copies ran while one was open for 24% of the time, Pallas kernels for 0%

profile of v1, /device:TPU:0, one launch (start us, length us, event | category | flops | bytes accessed | tf_op | source)
XLA Modules:
  0.0 1028.8 jit_solution(15409342507324348460)
XLA Ops:
  9.4 4.1 collective-permute-start.1
  34.5 2.6 slice.587
  37.2 2.7 slice.576
  39.8 2.7 slice.581
  42.5 2.7 slice.589
  90.0 4.6 pad.263
  104.1 4.6 pad.260
  112.9 8.9 rev.34
  121.8 5.2 rev.41
  127.1 176.6 %all-gather.4 = f32[64,1,1024]{2,1,0:T(1,128)S(1)} all-gather(f32[1,1,1024]{2,1,0:T(1,128)S(1)} %get-tuple-element.198), channel_id=1, replica_groups=mesh['seq'=64,'ch'=2] {'seq'}, dimensions={0}, use_global_device_ids=true | all-gather | bytes 266240 | tf_op jit(solution)/shard_map/all_gather | solution.py:9
  303.7 2.6 rev.39
  306.3 170.6 %all-gather.3 = f32[64,1,1024]{2,1,0:T(1,128)S(1)} all-gather(f32[1,1,1024]{2,1,0:T(1,128)S(1)} %get-tuple-element.199), channel_id=1, replica_groups=mesh['seq'=64,'ch'=2] {'seq'}, dimensions={0}, use_global_device_ids=true | all-gather | bytes 266240 | tf_op jit(solution)/shard_map/all_gather | solution.py:9
  477.0 2.6 rev.38
  480.1 5.2 rev.40
  485.3 172.6 %all-gather.2 = f32[64,1,1024]{2,1,0:T(1,128)S(1)} all-gather(f32[1,1,1024]{2,1,0:T(1,128)S(1)} %get-tuple-element.200), channel_id=1, replica_groups=mesh['seq'=64,'ch'=2] {'seq'}, dimensions={0}, use_global_device_ids=true | all-gather | bytes 266240 | tf_op jit(solution)/shard_map/all_gather | solution.py:9
  660.5 170.6 %all-gather.1 = f32[64,1,1024]{2,1,0:T(1,128)S(1)} all-gather(f32[1,1,1024]{2,1,0:T(1,128)S(1)} %get-tuple-element.201), channel_id=1, replica_groups=mesh['seq'=64,'ch'=2] {'seq'}, dimensions={0}, use_global_device_ids=true | all-gather | bytes 266240 | tf_op jit(solution)/shard_map/all_gather | solution.py:9
  833.7 102.7 %while.16 = (s32[]{:T(128)}, f32[1024]{0:T(1024)S(1)}, f32[1024]{0:T(1024)S(1)}, s32[]{:T(128)}, f32[64,1024]{1,0:T(8,128)}, /*index=5*/f32[64,1024]{1,0:T(8,128...) while((s32[]{:T(128)}, f32[1024]{0:T(1024)S(1)}, f32[1024]{0:T(1024)S(1)}, ...), condition=%wide.region_1.2_spmd.clone, body=%wide.region_0.1_spmd.clone.sunk | while | flops 12292 | bytes 65673 | solution.py:20
  943.8 2.6 collective-permute-done
  948.3 8.0 fusion.11
  957.2 12.7 %fusion.5 = bf16[256,4096]{1,0:T(8,128)(2,1)} fusion(bf16[4096,2,1024]{2,1,0:T(2,128)(2,1)} %param.13, bf16[256,2,1024]{2,1,0:T(2,128)(2,1)S(1)} %get-tuple-element.208), kind=kOutput, calls=%fused_computation.9 | convolution fusion | flops 4296015872 | bytes 19922944 | tf_op jit(solution)/shard_map/dot_general | solution.py:97
  969.9 2.6 copy.31
  972.6 19.3 %all_to_all.18 = bf16[2,1024,256]{2,0,1:T(2,128)(2,1)S(1)} all-to-all(bf16[2,1024,256]{2,0,1:T(2,128)(2,1)S(1)} %copy.31), channel_id=1, replica_groups=mesh['seq'=64,'ch'=2] {'seq'}, dimensions={1} | all-to-all | bytes 2097152 | tf_op jit(solution)/shard_map/all_to_all | solution.py:95
  993.0 25.5 %all-gather.7.cloned.1.call-done = f32[256,2,1024]{2,1,0:T(2,128)} async-done(((f32[4,2,1024]{2,1,0:T(2,128)}), f32[256,2,1024]{2,1,0:T(2,128)}) %all-gather.7.cloned.1.call-update) | async-done | bytes 2097168 | tf_op jit(solution)/shard_map/all_gather | solution.py:93
  1018.5 2.9 reduce_sum.49
  (552 shorter events, 197.2 us)
Async XLA Ops:
  8.0 1010.5 %all-gather.7.cloned.1.call-start = ((), (), s32[]{:S(2)}) async-start(), calls=%async_computation.3 | async-start | bytes 2129920 | tf_op jit(solution)/shard_map/all_gather | solution.py:93
  9.4 932.6 %collective-permute-start.1 = (bf16[3,2,1024]{2,1,0:T(2,128)(2,1)}, bf16[3,2,1024]{2,1,0:T(2,128)(2,1)}, u32[]{:S(2)}, u32[]{:S(2)}) collective-permute-start(bf16[3,2,1024]{2,1,0:T(2,128)(2,1)} %slice.741), channel_id=1, source_target_pairs={{0,2},{2,4},{4,6},{6,8},{8,10},{10,12},{12,14},{14,16},{16,18},{18... | collective-permute-start | bytes 36872 | tf_op jit(solution)/shard_map/ppermute | solution.py:26
  15.5 5.6 copy-start.5
  21.3 4.4 copy-start.24
  30.0 4.5 copy-start.19
  30.1 7.1 copy-start.18
  34.5 5.3 copy-start.21
  34.5 8.0 copy-start.20
  62.9 4.8 copy-start.33
  63.6 4.0 copy-start.35
  63.6 4.0 copy-start.39
  68.5 4.0 copy-start.25
  68.5 4.0 copy-start.26
  72.8 4.2 copy-start.30
  72.8 5.8 copy-start.29
  75.2 5.2 copy-start.28
  75.2 5.2 copy-start.27
  111.8 10.0 copy-start.6
  121.8 357.7 %copy-start.8 = (f32[256,1024]{1,0:T(8,128)S(1)}, f32[256,1024]{1,0:T(8,128)}, u32[]{:S(2)}) copy-start(f32[256,1024]{1,0:T(8,128)} %add.571) | copy-start | bytes 3145732
  303.7 176.4 %copy-start.7 = (f32[256,1024]{1,0:T(8,128)S(1)}, f32[256,1024]{1,0:T(8,128)}, u32[]{:S(2)}) copy-start(f32[256,1024]{1,0:T(8,128)} %add.573) | copy-start | bytes 3145732
  485.3 451.1 %copy-start.9 = (f32[256,1024]{1,0:T(8,128)S(1)}, f32[256,1024]{1,0:T(8,128)}, u32[]{:S(2)}) copy-start(f32[256,1024]{1,0:T(8,128)} %rev.34) | copy-start | bytes 3145732
  485.3 451.1 %copy-start.10 = (f32[256,1024]{1,0:T(8,128)S(1)}, f32[256,1024]{1,0:T(8,128)}, u32[]{:S(2)}) copy-start(f32[256,1024]{1,0:T(8,128)} %rev.41) | copy-start | bytes 3145732
  940.6 5.7 collective-permute-start
  956.9 64.4 %reduce-scatter.2.cloned.1.call-start = ((), (), s32[]{:S(2)}) async-start(), calls=%async_computation.2 | async-start | bytes 3145728 | tf_op jit(solution)/shard_map/reduce_scatter | solution.py:96
  (23 other events, 42.5 us)
Sparse Core Ops, SparseCore 0:
  957.1 61.3 all-gather.6
Sparse Core Ops, SparseCore 1:
  970.0 7.7 reduce-scatter.1
